TPU v7x, 32 devices: a whole 2x2x4 slice. The times are simulated.
32 devices in a mesh: dp: 2 (over core), blk: 4 (over y, x), head: 4 (over z).
Axes of the slice: x: 2, y: 2, z: 4, core: 2. Of those that a mesh axis runs over, the one named last changes fastest.
Arguments:
- activations: bfloat16 [2, 2, 2048, 1536], P(None, 'dp', ('blk', 'head')), may hold values from -6 to 6
- segments: int32 [2, 2, 2048], P(None, 'dp', 'blk'), may hold values from 0 to 15, never falling along the last dimension, each value on 1 to 1024 neighbouring positions
- cotangent: bfloat16 [2, 2, 2048, 1536], P(None, 'dp', ('blk', 'head')), may hold values from -6 to 6
- norm_gain_one: bfloat16 [1536], P(('dp', 'blk')), may hold values from 0.5 to 1.5
- query_weight: bfloat16 [1536, 1536], P(('dp', 'blk')), may hold values from -0.15625 to 0.15625
- key_weight: bfloat16 [1536, 768], P(('dp', 'blk')), may hold values from -0.15625 to 0.15625
- value_weight: bfloat16 [1536, 768], P(('dp', 'blk')), may hold values from -0.15625 to 0.15625
- output_weight: bfloat16 [1536, 1536], P(('dp', 'blk')), may hold values from -1.25 to 1.25
- norm_gain_two: bfloat16 [1536], P(('dp', 'blk')), may hold values from 0.5 to 1.5
- gate_weight: bfloat16 [1536, 4096], P(('dp', 'blk')), may hold values from -0.15625 to 0.15625
- up_weight: bfloat16 [1536, 4096], P(('dp', 'blk')), may hold values from -0.15625 to 0.15625
- down_weight: bfloat16 [4096, 1536], P(('dp', 'blk')), may hold values from -0.09375 to 0.09375
Outputs:
- block_out: bfloat16 [2, 2, 2048, 1536], P(None, 'dp', ('blk', 'head'))
- grad_input: bfloat16 [2, 2, 2048, 1536], P(None, 'dp', ('blk', 'head'))
- grad_gain_one: float32 [1536], P(('dp', 'blk'))
- grad_query: float32 [1536, 1536], P(('dp', 'blk'))
- grad_key: float32 [1536, 768], P(('dp', 'blk'))
- grad_value: float32 [1536, 768], P(('dp', 'blk'))
- grad_output: float32 [1536, 1536], P(('dp', 'blk'))
- grad_gain_two: float32 [1536], P(('dp', 'blk'))
- grad_gate: float32 [1536, 4096], P(('dp', 'blk'))
- grad_up: float32 [1536, 4096], P(('dp', 'blk'))
- grad_down: float32 [4096, 1536], P(('dp', 'blk'))
Inputs may be any that keep to these rules, and one draw needn't show every extreme that they name: `segments`: along each sequence the segment numbers never fall and every number is used; a document has at most 1024 tokens, and in every sequence one has exactly that many.
All inputs are finite; a program needn't handle non-finite values.
Results may differ from a plain program's by a relative error of at most 0.023.
Values may be sent and summed in bfloat16 or wider, within the bound.
No kernel may reach another device: no remote copies, remote signals or barrier semaphores. Data moves between devices by JAX's collectives and lax.ppermute only.
A program may use at most 320 MiB of HBM per device.

v0:
```python
import math
import jax
import jax.numpy as jnp
from jax import lax
from jax.sharding import PartitionSpec as P

D = 1536
QH = 16
KVH = 8
HD = 96
FF = 4096
EPS = 1e-05
NEG = -1e30


def shortened(value):
    return jax.tree.map(lambda a: a.astype(jnp.bfloat16) if a.dtype == jnp.float32 else a, value)


def plain_dot(left, right):
    return jnp.dot(left, right, preferred_element_type=jnp.float32)


def first_dot(left, right):
    return lax.dot_general(
        left, right, (((0,), (0,)), ((), ())), preferred_element_type=jnp.float32
    )


def last_dot(left, right):
    return lax.dot_general(
        left, right, (((1,), (1,)), ((), ())), preferred_element_type=jnp.float32
    )


def normalize(values):
    factor = lax.rsqrt(jnp.mean(values * values, -1, keepdims=True) + EPS)
    return (values * factor, factor)


def norm_back(grad_norm, gain, normed, factor):
    scaled = grad_norm * gain
    return factor * (scaled - normed * jnp.mean(scaled * normed, -1, keepdims=True))


def per_device(
    activations,
    segments,
    cotangent,
    norm_gain_one,
    query_weight,
    key_weight,
    value_weight,
    output_weight,
    norm_gain_two,
    gate_weight,
    up_weight,
    down_weight,
):
    shards = (
        norm_gain_one,
        query_weight,
        key_weight,
        value_weight,
        output_weight,
        norm_gain_two,
        gate_weight,
        up_weight,
        down_weight,
    )
    head_count = lax.axis_size("head")
    cycle_count = lax.axis_size("blk")
    tok_rows = activations.shape[2]
    span_len = tok_rows * head_count
    seq_len = span_len * cycle_count
    heads_here = QH // head_count
    kv_repeat = max(1, head_count // KVH)
    kv_here = KVH * kv_repeat // head_count
    group_size = heads_here // kv_here
    block_rows = span_len if span_len <= 1024 else 1024
    block_count = span_len // block_rows
    scale = 1.0 / math.sqrt(HD)
    first_pos = lax.axis_index("blk") * span_len
    full_shapes = (
        (D,),
        (D, QH * HD),
        (D, KVH * HD),
        (D, KVH * HD),
        (QH * HD, D),
        (D,),
        (D, FF),
        (D, FF),
        (FF, D),
    )
    totals = tuple((jnp.zeros(shape_full, jnp.float32) for shape_full in full_shapes))
    results = []
    grads_x = []
    for batch_index in range(activations.shape[0]):
        seg_rows = segments[batch_index, 0]
        cot_rows = cotangent[batch_index, 0]
        gain_one = lax.all_gather(shards[0], ("dp", "blk"), axis=0, tiled=True)
        query_w = lax.all_gather(shards[1], ("dp", "blk"), axis=0, tiled=True)
        key_w = lax.all_gather(shards[2], ("dp", "blk"), axis=0, tiled=True)
        value_w = lax.all_gather(shards[3], ("dp", "blk"), axis=0, tiled=True)
        out_w = lax.all_gather(shards[4], ("dp", "blk"), axis=0, tiled=True)
        gain_two = lax.all_gather(shards[5], ("dp", "blk"), axis=0, tiled=True)
        gate_w = lax.all_gather(shards[6], ("dp", "blk"), axis=0, tiled=True)
        up_w = lax.all_gather(shards[7], ("dp", "blk"), axis=0, tiled=True)
        down_w = lax.all_gather(shards[8], ("dp", "blk"), axis=0, tiled=True)
        gain_one_f = gain_one.astype(jnp.float32)
        gain_two_f = gain_two.astype(jnp.float32)
        x_float = activations[batch_index, 0].astype(jnp.float32)
        normed_one, factor_one = normalize(x_float)
        input_one = (normed_one * gain_one_f).astype(jnp.bfloat16)
        queries = plain_dot(input_one, query_w).astype(jnp.bfloat16).reshape(tok_rows, QH, HD)
        keys = plain_dot(input_one, key_w).astype(jnp.bfloat16).reshape(tok_rows, KVH, HD)
        values = plain_dot(input_one, value_w).astype(jnp.bfloat16).reshape(tok_rows, KVH, HD)
        if kv_repeat > 1:
            keys = jnp.repeat(keys, kv_repeat, axis=1)
            values = jnp.repeat(values, kv_repeat, axis=1)
        head_q = lax.all_to_all(queries, "head", split_axis=1, concat_axis=0, tiled=True)
        head_k = lax.all_to_all(keys, "head", split_axis=1, concat_axis=0, tiled=True)
        head_v = lax.all_to_all(values, "head", split_axis=1, concat_axis=0, tiled=True)
        query_blocks = head_q.reshape(block_count, block_rows, kv_here, group_size, HD)
        pos_blocks = (first_pos + jnp.arange(span_len, dtype=jnp.int32)).reshape(
            block_count, block_rows
        )
        seg_blocks = seg_rows.reshape(block_count, block_rows)
        key_piece = lax.all_gather(head_k, "blk", axis=0, tiled=True)
        value_piece = lax.all_gather(head_v, "blk", axis=0, tiled=True)
        seg_piece = lax.all_gather(seg_rows, "blk", axis=0, tiled=True)
        key_pos = jnp.arange(key_piece.shape[0], dtype=jnp.int32)

        def one_block(inputs):
            query_blk, query_pos, query_seg, run_max, run_sum, run_acc = inputs
            scores = (
                jnp.einsum(
                    "qhrd,khd->hrqk", query_blk, key_piece, preferred_element_type=jnp.float32
                )
                * scale
            )
            allowed = (key_pos[None, :] <= query_pos[:, None]) & (
                seg_piece[None, :] == query_seg[:, None]
            )
            new_max = jnp.maximum(run_max, jnp.max(jnp.where(allowed, scores, NEG), axis=-1))
            expo = jnp.where(allowed, jnp.exp(scores - new_max[..., None]), 0.0)
            decay = jnp.exp(run_max - new_max)
            new_sum = run_sum * decay + jnp.sum(expo, -1)
            new_acc = run_acc * decay[..., None] + jnp.einsum(
                "hrqk,khd->hrqd",
                expo.astype(jnp.bfloat16),
                value_piece,
                preferred_element_type=jnp.float32,
            )
            return (new_max, new_sum, new_acc)

        run_max, run_sum, run_acc = lax.map(
            one_block,
            (
                query_blocks,
                pos_blocks,
                seg_blocks,
                jnp.full((block_count, kv_here, group_size, block_rows), NEG, jnp.float32),
                jnp.zeros((block_count, kv_here, group_size, block_rows), jnp.float32),
                jnp.zeros((block_count, kv_here, group_size, block_rows, HD), jnp.float32),
            ),
        )
        attn_heads = run_acc / run_sum[..., None]
        log_total = run_max + jnp.log(run_sum)
        attn_low = (
            attn_heads.transpose(0, 3, 1, 2, 4)
            .reshape(span_len, heads_here, HD)
            .astype(jnp.bfloat16)
        )
        attn_tok = lax.all_to_all(
            attn_low, "head", split_axis=0, concat_axis=1, tiled=True
        ).reshape(tok_rows, QH * HD)
        x_mid = x_float + plain_dot(attn_tok, out_w)
        normed_two, factor_two = normalize(x_mid)
        input_two = (normed_two * gain_two_f).astype(jnp.bfloat16)
        gate_val = plain_dot(input_two, gate_w)
        up_val = plain_dot(input_two, up_w)
        sigma = jax.nn.sigmoid(gate_val)
        silu_val = gate_val * sigma
        hidden = (silu_val * up_val).astype(jnp.bfloat16)
        result = (x_mid + plain_dot(hidden, down_w)).astype(jnp.bfloat16)
        grad_down = first_dot(hidden, cot_rows)
        grad_hidden = last_dot(cot_rows, down_w)
        grad_gate_val = (grad_hidden * up_val * sigma * (1.0 + gate_val * (1.0 - sigma))).astype(
            jnp.bfloat16
        )
        grad_up_val = (grad_hidden * silu_val).astype(jnp.bfloat16)
        grad_gate_w = first_dot(input_two, grad_gate_val)
        grad_up_w = first_dot(input_two, grad_up_val)
        grad_input_two = last_dot(grad_gate_val, gate_w) + last_dot(grad_up_val, up_w)
        grad_gain_two = jnp.sum(grad_input_two * normed_two, 0)
        grad_mid = cot_rows.astype(jnp.float32) + norm_back(
            grad_input_two, gain_two_f, normed_two, factor_two
        )
        grad_branch = grad_mid.astype(jnp.bfloat16)
        grad_out_w = first_dot(attn_tok, grad_branch)
        grad_attn = last_dot(grad_branch, out_w).astype(jnp.bfloat16).reshape(tok_rows, QH, HD)
        grad_heads = lax.all_to_all(grad_attn, "head", split_axis=1, concat_axis=0, tiled=True)
        grad_blocks = grad_heads.reshape(block_count, block_rows, kv_here, group_size, HD)
        delta = jnp.sum(grad_blocks.astype(jnp.float32).transpose(0, 2, 3, 1, 4) * attn_heads, -1)
        full_k = lax.all_gather(head_k, "blk", axis=0, tiled=True)
        full_v = lax.all_gather(head_v, "blk", axis=0, tiled=True)
        full_seg = lax.all_gather(seg_rows, "blk", axis=0, tiled=True)
        key_k = full_k.reshape(cycle_count, span_len, kv_here, HD)
        key_v = full_v.reshape(cycle_count, span_len, kv_here, HD)
        key_seg = full_seg.reshape(cycle_count, span_len)
        key_pos = jnp.arange(seq_len, dtype=jnp.int32).reshape(cycle_count, span_len)

        def key_step(grad_total, key_inputs):
            blk_k, blk_v, blk_seg, blk_pos = key_inputs

            def query_step(carry, inputs):
                sum_k, sum_v = carry
                query_blk, query_pos, query_seg, lse_blk, delta_blk, grad_blk = inputs
                scores = (
                    jnp.einsum(
                        "qhrd,khd->hrqk", query_blk, blk_k, preferred_element_type=jnp.float32
                    )
                    * scale
                )
                allowed = (blk_pos[None, :] <= query_pos[:, None]) & (
                    blk_seg[None, :] == query_seg[:, None]
                )
                probs = jnp.where(allowed, jnp.exp(scores - lse_blk[..., None]), 0.0)
                grad_probs = jnp.einsum(
                    "qhrd,khd->hrqk", grad_blk, blk_v, preferred_element_type=jnp.float32
                )
                grad_scores = (probs * (grad_probs - delta_blk[..., None])).astype(jnp.bfloat16)
                grad_query = (
                    jnp.einsum(
                        "hrqk,khd->qhrd", grad_scores, blk_k, preferred_element_type=jnp.float32
                    )
                    * scale
                )
                sum_k = (
                    sum_k
                    + jnp.einsum(
                        "hrqk,qhrd->khd", grad_scores, query_blk, preferred_element_type=jnp.float32
                    )
                    * scale
                )
                sum_v = sum_v + jnp.einsum(
                    "hrqk,qhrd->khd",
                    probs.astype(jnp.bfloat16),
                    grad_blk,
                    preferred_element_type=jnp.float32,
                )
                return ((sum_k, sum_v), grad_query)

            empty_kv = jnp.zeros((span_len, kv_here, HD), jnp.float32)
            (sum_k, sum_v), grad_part = lax.scan(
                query_step,
                (empty_kv, empty_kv),
                (query_blocks, pos_blocks, seg_blocks, log_total, delta, grad_blocks),
            )
            return (grad_total + grad_part, (sum_k, sum_v))

        grad_start = jnp.zeros((block_count, block_rows, kv_here, group_size, HD), jnp.float32)
        grad_query, (sums_k, sums_v) = lax.scan(
            key_step, grad_start, (key_k, key_v, key_seg, key_pos)
        )
        sum_k = sums_k.reshape(seq_len, kv_here, HD)
        sum_v = sums_v.reshape(seq_len, kv_here, HD)
        owned_k = lax.psum_scatter(
            sum_k.astype(jnp.bfloat16), "blk", scatter_dimension=0, tiled=True
        ).astype(jnp.float32)
        owned_v = lax.psum_scatter(
            sum_v.astype(jnp.bfloat16), "blk", scatter_dimension=0, tiled=True
        ).astype(jnp.float32)
        grad_query = grad_query.reshape(span_len, heads_here, HD)
        tok_q = lax.all_to_all(
            grad_query.astype(jnp.bfloat16), "head", split_axis=0, concat_axis=1, tiled=True
        ).astype(grad_query.dtype)
        tok_k = lax.all_to_all(
            owned_k.astype(jnp.bfloat16), "head", split_axis=0, concat_axis=1, tiled=True
        ).astype(owned_k.dtype)
        tok_v = lax.all_to_all(
            owned_v.astype(jnp.bfloat16), "head", split_axis=0, concat_axis=1, tiled=True
        ).astype(owned_v.dtype)
        tok_q = tok_q.reshape(tok_rows, QH * HD).astype(jnp.bfloat16)
        tok_k = (
            jnp.sum(tok_k.reshape(tok_rows, KVH, kv_repeat, HD), 2)
            .reshape(tok_rows, KVH * HD)
            .astype(jnp.bfloat16)
        )
        tok_v = (
            jnp.sum(tok_v.reshape(tok_rows, KVH, kv_repeat, HD), 2)
            .reshape(tok_rows, KVH * HD)
            .astype(jnp.bfloat16)
        )
        grad_query_w = first_dot(input_one, tok_q)
        grad_key_w = first_dot(input_one, tok_k)
        grad_value_w = first_dot(input_one, tok_v)
        grad_input_one = (
            last_dot(tok_q, query_w) + last_dot(tok_k, key_w) + last_dot(tok_v, value_w)
        )
        grad_gain_one = jnp.sum(grad_input_one * normed_one, 0)
        grad_x = (grad_mid + norm_back(grad_input_one, gain_one_f, normed_one, factor_one)).astype(
            jnp.bfloat16
        )
        result, grad_x, terms = (
            result,
            grad_x,
            (
                grad_gain_one,
                grad_query_w,
                grad_key_w,
                grad_value_w,
                grad_out_w,
                grad_gain_two,
                grad_gate_w,
                grad_up_w,
                grad_down,
            ),
        )
        results.append(result)
        grads_x.append(grad_x)
        totals = tuple((left + right for left, right in zip(totals, terms)))
    owned = jax.tree.map(
        lambda part: part.astype(jnp.float32),
        lax.psum_scatter(shortened(totals), ("dp", "blk"), scatter_dimension=0, tiled=True),
    )
    owned = jax.tree.map(lambda part: part.astype(jnp.float32), lax.psum(shortened(owned), "head"))
    block_out = jnp.stack(results)[:, None]
    grad_input = jnp.stack(grads_x)[:, None]
    return (
        block_out,
        grad_input,
        owned[0],
        owned[1],
        owned[2],
        owned[3],
        owned[4],
        owned[5],
        owned[6],
        owned[7],
        owned[8],
    )


def solution(mesh):
    placed = (
        P(None, "dp", ("blk", "head"), None),
        P(None, "dp", "blk"),
        P(None, "dp", ("blk", "head"), None),
        P(("dp", "blk")),
        P(("dp", "blk"), None),
        P(("dp", "blk"), None),
        P(("dp", "blk"), None),
        P(("dp", "blk"), None),
        P(("dp", "blk")),
        P(("dp", "blk"), None),
        P(("dp", "blk"), None),
        P(("dp", "blk"), None),
    )
    return jax.shard_map(
        per_device,
        mesh=mesh,
        in_specs=placed,
        out_specs=(
            P(None, "dp", ("blk", "head"), None),
            P(None, "dp", ("blk", "head"), None),
            P(("dp", "blk")),
            P(("dp", "blk"), None),
            P(("dp", "blk"), None),
            P(("dp", "blk"), None),
            P(("dp", "blk"), None),
            P(("dp", "blk")),
            P(("dp", "blk"), None),
            P(("dp", "blk"), None),
            P(("dp", "blk"), None),
        ),
        check_vma=False,
    )
```

profile of v0, /device:TPU:0, one launch (start us, length us, event | category | flops | bytes accessed | tf_op | source)
XLA Modules:
  0.0 1429.7 jit_solution(12849763053035598999)
XLA Ops:
  13.7 16.3 %all-reduce.5 = (bf16[1536]{0:T(1024)(128)(2,1)S(1)}, bf16[1536]{0:T(1024)(128)(2,1)S(1)}) all-reduce(bf16[1536]{0:T(1024)(128)(2,1)S(1)} %dynamic-update-slice, bf16[1536]{0:T(1024)(128)(2,1)S(1)} %dynamic-update-slice.1), channel_id=1, replica_groups=mesh['dp'=2,'blk'=4,'head'=4] {'dp','blk'}, use_global_device_ids=true, to_apply=%add | all-reduce | flops 3072 | bytes 12288
  57.7 15.3 %all-gather.14.cloned.1.call-done = bf16[1536,768]{1,0:T(8,128)(2,1)} async-done(((bf16[192,768]{1,0:T(8,128)(2,1)}), bf16[1536,768]{1,0:T(8,128)(2,1)}) %all-gather.14.cloned.1.call-update) | async-done | bytes 2359312 | tf_op jit(solution)/shard_map/all_gather | solution.py:104
  105.3 13.9 all_gather.73
  119.2 14.7 %all_gather.74 = bf16[2048,2,96]{0,2,1:T(8,128)(2,1)} all-gather(bf16[512,2,96]{0,2,1:T(8,128)(2,1)S(1)} %all_to_all.220), channel_id=1, replica_groups=mesh['dp'=2,'blk'=4,'head'=4] {'blk'}, dimensions={0}, use_global_device_ids=true | all-gather | bytes 983040 | tf_op jit(solution)/shard_map/all_gather | solution.py:130
  144.3 20.2 %all_gather.63 = bf16[2048,2,96]{0,2,1:T(8,128)(2,1)} all-gather(bf16[512,2,96]{0,2,1:T(8,128)(2,1)S(1)} %all_to_all.199), channel_id=1, replica_groups=mesh['dp'=2,'blk'=4,'head'=4] {'blk'}, dimensions={0}, use_global_device_ids=true | all-gather | bytes 983040 | tf_op jit(solution)/shard_map/all_gather | solution.py:129
  164.8 11.4 all_gather.66
  258.6 55.3 %all-gather.20.cloned.1.call-done = bf16[1536,4096]{1,0:T(8,128)(2,1)} async-done(((bf16[192,4096]{1,0:T(8,128)(2,1)}), bf16[1536,4096]{1,0:T(8,128)(2,1)}) %all-gather.20.cloned.1.call-update) | async-done | bytes 12582928 | tf_op jit(solution)/shard_map/all_gather | solution.py:108
  321.6 66.3 %all-gather.22.cloned.1.call-done = bf16[4096,1536]{1,0:T(8,128)(2,1)} async-done(((bf16[512,1536]{1,0:T(8,128)(2,1)}), bf16[4096,1536]{1,0:T(8,128)(2,1)}) %all-gather.22.cloned.1.call-update) | async-done | bytes 12582928 | tf_op jit(solution)/shard_map/all_gather | solution.py:109
  387.9 11.4 multiply_convert_fusion.2
  399.4 10.5 fusion.214
  409.9 11.6 multiply_reduce_fusion.1
  432.2 9.9 multiply_convert_fusion
  489.3 50.1 %while.25 = (s32[]{:T(128)}, f32[1,512,2,2,96]{1,4,3,2,0:T(8,128)}, bf16[4,512,2,96]{1,3,2,0:T(8,128)(2,1)}, bf16[4,512,2,96]{1,3,2,0:T(8,128)(2,1)}, bf16[4,512...) while((s32[]{:T(128)}, f32[1,512,2,2,96]{1,4,3,2,0:T(8,128)}, ...), condition=%wide.region_18.19_spmd.clone, body=%wide.region_17.18_spmd.clone.sunk | while | flops 1018593792 | bytes 67217776 | solution.py:264
  545.2 46.2 %while.24 = (s32[]{:T(128)}, f32[1,512,2,2,96]{1,4,3,2,0:T(8,128)S(1)}, bf16[4,512,2,96]{1,3,2,0:T(8,128)(2,1)}, bf16[4,512,2,96]{1,3,2,0:T(8,128)(2,1)}, bf16[4...) while((s32[]{:T(128)}, ...), condition=%wide.region_11.12_spmd.clone, body=%wide.region_10.11_spmd.clone.sunk | while | flops 1018593792 | bytes 69314976 | solution.py:264
  604.0 16.3 %reduce-scatter.12.cloned.1.call-done = bf16[512,2,96]{0,2,1:T(8,128)(2,1)} async-done(((bf16[2048,2,96]{0,2,1:T(8,128)(2,1)}), bf16[512,2,96]{0,2,1:T(8,128)(2,1)}) %reduce-scatter.12.cloned.1.call-update) | async-done | bytes 196624 | tf_op jit(solution)/shard_map/reduce_scatter | solution.py:269
  639.1 10.6 reduce-scatter.18.cloned.1.call-done
  656.2 22.6 %reduce-scatter.14.cloned.1.call-done = bf16[512,2,96]{0,2,1:T(8,128)(2,1)} async-done(((bf16[2048,2,96]{0,2,1:T(8,128)(2,1)}), bf16[512,2,96]{0,2,1:T(8,128)(2,1)}) %reduce-scatter.14.cloned.1.call-update) | async-done | bytes 196624 | tf_op jit(solution)/shard_map/reduce_scatter | solution.py:272
  710.1 11.7 all-to-all-done.13
  725.7 12.8 all-to-all-done.9
  745.0 11.8 fusion.218
  756.8 14.7 %add_convert_fusion.2 = bf16[1536,4096]{1,0:T(8,128)(2,1)} fusion(f32[1536,4096]{1,0:T(8,128)} %fusion.218, bf16[128,1536]{1,0:T(8,128)(2,1)S(1)} %copy-done.16, bf16[128,4096]{1,0:T(8,128)(2,1)S(1)} %copy-done.37), kind=kOutput, calls=%fused_computation.80 | convolution fusion | flops 1623195648 | bytes 39190528 | tf_op jit(solution)/shard_map/dot_general | solution.py:25
  771.7 12.2 fusion.219
  783.9 16.2 %add_convert_fusion.1 = bf16[1536,4096]{1,0:T(8,128)(2,1)} fusion(f32[1536,4096]{1,0:T(8,128)} %fusion.219, bf16[128,1536]{1,0:T(8,128)(2,1)S(1)} %copy-done.16, bf16[128,4096]{1,0:T(8,128)(2,1)S(1)} %copy-done.35), kind=kOutput, calls=%fused_computation.79 | convolution fusion | flops 1623195648 | bytes 39190528 | tf_op jit(solution)/shard_map/dot_general | solution.py:25
  801.2 11.9 fusion.165
  813.2 15.4 %add_convert_fusion = bf16[4096,1536]{1,0:T(8,128)(2,1)} fusion(f32[4096,1536]{1,0:T(8,128)} %fusion.165, bf16[128,4096]{1,0:T(8,128)(2,1)S(1)} %copy-done.25, bf16[2,1,128,1536]{3,2,1,0:T(8,128)(2,1)S(1)} %copy-done.45), kind=kOutput, calls=%fused_computation.78 | convolution fusion | flops 1623195648 | bytes 39190528 | tf_op jit(solution)/shard_map/dot_general | solution.py:25
  829.1 57.6 %reduce-scatter.20.cloned.1.call-done = bf16[192,1536]{1,0:T(8,128)(2,1)} async-done(((bf16[1536,1536]{1,0:T(8,128)(2,1)}), bf16[192,1536]{1,0:T(8,128)(2,1)}) %reduce-scatter.20.cloned.1.call-update) | async-done | bytes 589840 | tf_op jit(solution)/shard_map/reduce_scatter | solution.py:326
  886.7 95.8 %reduce-scatter.28.cloned.1.call-done = bf16[192,4096]{1,0:T(8,128)(2,1)} async-done(((bf16[1536,4096]{1,0:T(8,128)(2,1)}), bf16[192,4096]{1,0:T(8,128)(2,1)}) %reduce-scatter.28.cloned.1.call-update) | async-done | bytes 1572880 | tf_op jit(solution)/shard_map/reduce_scatter | solution.py:326
  982.4 95.8 %reduce-scatter.30.cloned.1.call-done = bf16[192,4096]{1,0:T(8,128)(2,1)} async-done(((bf16[1536,4096]{1,0:T(8,128)(2,1)}), bf16[192,4096]{1,0:T(8,128)(2,1)}) %reduce-scatter.30.cloned.1.call-update) | async-done | bytes 1572880 | tf_op jit(solution)/shard_map/reduce_scatter | solution.py:326
  1078.2 95.8 %reduce-scatter.32.cloned.1.call-done = bf16[512,1536]{1,0:T(8,128)(2,1)} async-done(((bf16[4096,1536]{1,0:T(8,128)(2,1)}), bf16[512,1536]{1,0:T(8,128)(2,1)}) %reduce-scatter.32.cloned.1.call-update) | async-done | bytes 1572880 | tf_op jit(solution)/shard_map/reduce_scatter | solution.py:326
  1198.1 14.9 %all-reduce.4 = (bf16[1536]{0:T(1024)(128)(2,1)S(1)}, bf16[1536]{0:T(1024)(128)(2,1)S(1)}) all-reduce(bf16[1536]{0:T(1024)(128)(2,1)S(1)} %add_convert_fusion.6, bf16[1536]{0:T(1024)(128)(2,1)S(1)} %add_convert_fusion.5), channel_id=8, replica_groups=mesh['dp'=2,'blk'=4,'head'=4] {'dp','blk'}, use_global_device_ids=true, to_apply=%region_24.25.clone | all-reduce | flops 3072 | bytes 12288
  1213.2 12.1 all-reduce.6
  1229.1 179.4 %all-reduce.10.cloned.1.call-done = (bf16[192,1536]{1,0:T(8,128)(2,1)}, bf16[192,768]{1,0:T(8,128)(2,1)}, bf16[192,768]{1,0:T(8,128)(2,1)}, bf16[192,1536]{1,0:T...) async-done(((bf16[192,1536]{1,0:T(8,128)(2,1)}, bf16[192,768]{1,0:T(8,128)(2,1)}, bf16[192,768]{1,0:T(8,128)(2,1)}, ...) | async-done | bytes 6488080 | tf_op jit(solution)/shard_map/psum | solution.py:328
  (567 shorter events, 446.9 us)
Async XLA Ops:
  7.2 42.5 %all-gather.10.cloned.1.call-start = ((), (), s32[]{:S(2)}) async-start(), calls=%async_computation.27 | async-start | bytes 2654208 | tf_op jit(solution)/shard_map/all_gather | solution.py:103
  8.0 65.1 %all-gather.14.cloned.1.call-start = ((), (), s32[]{:S(2)}) async-start(), calls=%async_computation.29 | async-start | bytes 2654208 | tf_op jit(solution)/shard_map/all_gather | solution.py:104
  8.7 125.2 %all-gather.12.cloned.1.call-start = ((), (), s32[]{:S(2)}) async-start(), calls=%async_computation.28 | async-start | bytes 5308416 | tf_op jit(solution)/shard_map/all_gather | solution.py:102
  9.5 234.9 %all-gather.16.cloned.1.call-start = ((), (), s32[]{:S(2)}) async-start(), calls=%async_computation.30 | async-start | bytes 5308416 | tf_op jit(solution)/shard_map/all_gather | solution.py:105
  10.0 240.1 %all-gather.18.cloned.1.call-start = ((), (), s32[]{:S(2)}) async-start(), calls=%async_computation.31 | async-start | bytes 14155776 | tf_op jit(solution)/shard_map/all_gather | solution.py:107
  10.6 303.3 %all-gather.20.cloned.1.call-start = ((), (), s32[]{:S(2)}) async-start(), calls=%async_computation.32 | async-start | bytes 14155776 | tf_op jit(solution)/shard_map/all_gather | solution.py:108
  11.2 376.8 %all-gather.22.cloned.1.call-start = ((), (), s32[]{:S(2)}) async-start(), calls=%async_computation.33 | async-start | bytes 14155776 | tf_op jit(solution)/shard_map/all_gather | solution.py:109
  52.8 25.0 %all-to-all-start.4 = ((bf16[128,8,96]{0,2,1:T(8,128)(2,1)}), bf16[128,8,96]{0,2,1:T(8,128)(2,1)S(1)}, u32[]{:S(2)}, u32[]{:S(2)}) async-start(bf16[128,8,96]{0,2,1:T(8,128)(2,1)} %bitcast.29), calls=%async_computation.4 | async-start | bytes 393216 | tf_op jit(solution)/shard_map/all_to_all | solution.py:122
  100.8 37.3 %all-to-all-start.2 = ((bf16[128,8,96]{0,2,1:T(8,128)(2,1)}), bf16[128,8,96]{0,2,1:T(8,128)(2,1)S(1)}, u32[]{:S(2)}, u32[]{:S(2)}) async-start(bf16[128,8,96]{0,2,1:T(8,128)(2,1)} %bitcast.13), calls=%async_computation.2 | async-start | bytes 393216 | tf_op jit(solution)/shard_map/all_to_all | solution.py:123
  138.0 44.7 %all-to-all-start.5 = ((bf16[128,16,96]{0,2,1:T(8,128)(2,1)}), bf16[128,16,96]{0,2,1:T(8,128)(2,1)S(1)}, u32[]{:S(2)}, u32[]{:S(2)}) async-start(bf16[128,16,96]{0,2,1:T(8,128)(2,1)} %bitcast.34), calls=%async_computation.5 | async-start | bytes 786432 | tf_op jit(solution)/shard_map/all_to_all | solution.py:121
  182.7 22.0 %all-to-all-start.1 = ((bf16[128,16,96]{0,2,1:T(8,128)(2,1)}), bf16[128,16,96]{0,2,1:T(8,128)(2,1)}, u32[]{:S(2)}, u32[]{:S(2)}) async-start(bf16[128,16,96]{0,2,1:T(8,128)(2,1)} %bitcast.9), calls=%async_computation.1 | async-start | bytes 786432 | tf_op jit(solution)/shard_map/all_to_all | solution.py:121
  204.7 22.1 %all-to-all-start.7 = ((bf16[512,4,96]{2,1,0:T(4,128)(2,1)}), bf16[512,4,96]{2,1,0:T(4,128)(2,1)S(1)}, u32[]{:S(2)}, u32[]{:S(2)}) async-start(bf16[512,4,96]{2,1,0:T(4,128)(2,1)} %copy.196), calls=%async_computation.7 | async-start | bytes 1048576 | tf_op jit(solution)/shard_map/all_to_all | solution.py:175
  226.8 16.0 %all-to-all-start.3 = ((bf16[512,4,96]{2,1,0:T(4,128)(2,1)}), bf16[512,4,96]{2,1,0:T(4,128)(2,1)}, u32[]{:S(2)}, u32[]{:S(2)}) async-start(bf16[512,4,96]{2,1,0:T(4,128)(2,1)} %copy.186), calls=%async_computation.3 | async-start | bytes 1048576 | tf_op jit(solution)/shard_map/all_to_all | solution.py:175
  464.8 16.7 %all-to-all-start.12 = ((bf16[128,16,96]{0,2,1:T(8,128)(2,1)}), bf16[128,16,96]{0,2,1:T(8,128)(2,1)S(1)}, u32[]{:S(2)}, u32[]{:S(2)}) async-start(bf16[128,16,96]{0,2,1:T(8,128)(2,1)} %bitcast.78), calls=%async_computation.14 | async-start | bytes 786432 | tf_op jit(solution)/shard_map/all_to_all | solution.py:203
  481.5 60.2 %all-to-all-start.8 = ((bf16[128,16,96]{0,2,1:T(8,128)(2,1)}), bf16[128,16,96]{0,2,1:T(8,128)(2,1)}, u32[]{:S(2)}, u32[]{:S(2)}) async-start(bf16[128,16,96]{0,2,1:T(8,128)(2,1)} %bitcast.57), calls=%async_computation.8 | async-start | bytes 786432 | tf_op jit(solution)/shard_map/all_to_all | solution.py:203
  485.6 111.4 %reduce-scatter.16.cloned.1.call-start = ((), (), s32[]{:S(2)}) async-start(), calls=%async_computation.36 | async-start | bytes 983040 | tf_op jit(solution)/shard_map/reduce_scatter | solution.py:269
  541.7 78.7 %reduce-scatter.12.cloned.1.call-start = ((), (), s32[]{:S(2)}) async-start(), calls=%async_computation.34 | async-start | bytes 983040 | tf_op jit(solution)/shard_map/reduce_scatter | solution.py:269
  593.7 56.1 %reduce-scatter.18.cloned.1.call-start = ((), (), s32[]{:S(2)}) async-start(), calls=%async_computation.37 | async-start | bytes 983040 | tf_op jit(solution)/shard_map/reduce_scatter | solution.py:272
  596.0 82.8 %reduce-scatter.14.cloned.1.call-start = ((), (), s32[]{:S(2)}) async-start(), calls=%async_computation.35 | async-start | bytes 983040 | tf_op jit(solution)/shard_map/reduce_scatter | solution.py:272
  598.9 23.3 %all-to-all-start.14 = ((bf16[512,2,96]{2,1,0:T(2,128)(2,1)}), bf16[512,2,96]{2,1,0:T(2,128)(2,1)S(1)}, u32[]{:S(2)}, u32[]{:S(2)}) async-start(bf16[512,2,96]{2,1,0:T(2,128)(2,1)} %copy.222), calls=%async_computation.17 | async-start | bytes 524288 | tf_op jit(solution)/shard_map/all_to_all | solution.py:279
  622.2 13.5 all-to-all-start.10
  626.7 202.2 %reduce-scatter.22.cloned.1.call-start = ((), (), s32[]{:S(2)}) async-start(), calls=%async_computation.39 | async-start | bytes 2654208 | tf_op jit(solution)/shard_map/reduce_scatter | solution.py:326
  651.6 29.0 %all-to-all-start.15 = ((bf16[512,2,96]{2,1,0:T(2,128)(2,1)}), bf16[512,2,96]{2,1,0:T(2,128)(2,1)S(1)}, u32[]{:S(2)}, u32[]{:S(2)}) async-start(bf16[512,2,96]{2,1,0:T(2,128)(2,1)} %copy.226), calls=%async_computation.19 | async-start | bytes 524288 | tf_op jit(solution)/shard_map/all_to_all | solution.py:282
  685.2 143.8 %reduce-scatter.24.cloned.1.call-start = ((), (), s32[]{:S(2)}) async-start(), calls=%async_computation.40 | async-start | bytes 2654208 | tf_op jit(solution)/shard_map/reduce_scatter | solution.py:326
  697.6 131.5 %reduce-scatter.26.cloned.1.call-start = ((), (), s32[]{:S(2)}) async-start(), calls=%async_computation.41 | async-start | bytes 5308416 | tf_op jit(solution)/shard_map/reduce_scatter | solution.py:326
  705.5 16.4 %all-to-all-start.13 = ((bf16[512,4,96]{2,1,0:T(4,128)(2,1)}), bf16[512,4,96]{2,1,0:T(4,128)(2,1)S(1)}, u32[]{:S(2)}, u32[]{:S(2)}) async-start(bf16[512,4,96]{2,1,0:T(4,128)(2,1)} %bitcast.83), calls=%async_computation.15 | async-start | bytes 1048576 | tf_op jit(solution)/shard_map/all_to_all | solution.py:276
  721.9 16.6 %all-to-all-start.9 = ((bf16[512,4,96]{2,1,0:T(4,128)(2,1)}), bf16[512,4,96]{2,1,0:T(4,128)(2,1)S(1)}, u32[]{:S(2)}, u32[]{:S(2)}) async-start(bf16[512,4,96]{2,1,0:T(4,128)(2,1)} %bitcast.62), calls=%async_computation.9 | async-start | bytes 1048576 | tf_op jit(solution)/shard_map/all_to_all | solution.py:276
  725.4 161.3 %reduce-scatter.20.cloned.1.call-start = ((), (), s32[]{:S(2)}) async-start(), calls=%async_computation.38 | async-start | bytes 5308416 | tf_op jit(solution)/shard_map/reduce_scatter | solution.py:326
  744.0 238.4 %reduce-scatter.28.cloned.1.call-start = ((), (), s32[]{:S(2)}) async-start(), calls=%async_computation.42 | async-start | bytes 14155776 | tf_op jit(solution)/shard_map/reduce_scatter | solution.py:326
  771.5 306.7 %reduce-scatter.30.cloned.1.call-start = ((), (), s32[]{:S(2)}) async-start(), calls=%async_computation.43 | async-start | bytes 14155776 | tf_op jit(solution)/shard_map/reduce_scatter | solution.py:326
  800.1 373.9 %reduce-scatter.32.cloned.1.call-start = ((), (), s32[]{:S(2)}) async-start(), calls=%async_computation.44 | async-start | bytes 14155776 | tf_op jit(solution)/shard_map/reduce_scatter | solution.py:326
  828.7 579.8 %all-reduce.10.cloned.1.call-start = ((), (), s32[]{:S(2)}) async-start(), calls=%async_computation.45 | async-start | bytes 12976128 | tf_op jit(solution)/shard_map/psum | solution.py:328
  (139 other events, 2642.1 us)
Sparse Core Ops, SparseCore 0:
  9.9 32.1 all-gather.9
  44.0 28.9 all-gather.13
  75.0 42.0 all-gather.11
  118.8 46.9 all-gather.15
  167.5 72.4 all-gather.17
  241.7 72.1 all-gather.19
  315.8 72.1 all-gather.21
  541.8 26.5 reduce-scatter.15
  593.8 26.4 reduce-scatter.11
  623.7 26.0 reduce-scatter.17
  652.7 26.0 reduce-scatter.13
  682.6 42.4 reduce-scatter.21
  729.4 42.4 reduce-scatter.23
  775.2 53.8 reduce-scatter.25
  832.8 53.8 reduce-scatter.19
  890.0 92.3 reduce-scatter.27
  985.8 92.3 reduce-scatter.29
  1081.6 92.3 reduce-scatter.31
  1176.9 231.5 all-reduce.9
where the time goes:
time: 1440 us; the launch traced here: 1430 us
  waiting for transfers between devices  770 us (53%)
  matrix products  342 us (24%)
  blocking collectives  119 us (8%)
  starting transfers between devices  74.8 us (5%)
  local copies, waits for them, and re-layouts  70.3 us (5%)
  other arithmetic  35.4 us (2%)
  between operations  16.9 us (1%)
    reduce_scatter x7, waiting for transfers between devices, per_device(): lax.psum_scatter(shortened(totals), ('dp', 'blk'), scatter_dimension=0, t...  345 us
    psum x1, waiting for transfers between devices, per_device(): lax.psum(shortened(owned), 'head')  179 us
    dot_general x14, matrix products, first_dot(): lax.dot_general(left, right, (((0,), (0,)), ((), ())), preferred_element_...  98.8 us
    dot_general x14, matrix products, last_dot(): lax.dot_general(left, right, (((1,), (1,)), ((), ())), preferred_element_...  76.6 us
    all_gather x1, waiting for transfers between devices, per_device(): down_w = lax.all_gather(shards[8], ('dp', 'blk'), axis=0, tiled=True)  66.3 us
    dot_general x14, matrix products, plain_dot(): return jnp.dot(left, right, preferred_element_type=jnp.float32)  63.4 us
    all_gather x1, waiting for transfers between devices, per_device(): up_w = lax.all_gather(shards[7], ('dp', 'blk'), axis=0, tiled=True)  55.3 us
    all_gather x2, blocking collectives, per_device(): key_piece = lax.all_gather(head_k, 'blk', axis=0, tiled=True)  34.2 us
  transfers between devices with their start and end apart: 35, of which 19 were waited for; matrix products, arithmetic and copies ran while one was open for 24% of the time, Pallas kernels for 0%

commit v1 on v0

--- a/solution.py
+++ b/solution.py
@@ -11,6 +11,9 @@
 FF = 4096
 EPS = 1e-05
 NEG = -1e30
+_check_surface = lambda page: jnp.concatenate(
+    lax.all_to_all(jnp.stack(jnp.split(page, lax.psum(1, "head"), axis=0), axis=0), "head", 0, 0), 1
+)
 
 
 def shortened(value):
@@ -273,9 +276,7 @@
             sum_v.astype(jnp.bfloat16), "blk", scatter_dimension=0, tiled=True
         ).astype(jnp.float32)
         grad_query = grad_query.reshape(span_len, heads_here, HD)
-        tok_q = lax.all_to_all(
-            grad_query.astype(jnp.bfloat16), "head", split_axis=0, concat_axis=1, tiled=True
-        ).astype(grad_query.dtype)
+        tok_q = _check_surface(grad_query.astype(jnp.bfloat16)).astype(grad_query.dtype)
         tok_k = lax.all_to_all(
             owned_k.astype(jnp.bfloat16), "head", split_axis=0, concat_axis=1, tiled=True
         ).astype(owned_k.dtype)

time: 1440 us -> 1440 us (level)
  transfers between devices with their start and end apart: 35 -> 35, of which waited for: 19 -> 19; matrix products, arithmetic and copies ran while one was open for 24% -> 25% of each run, Pallas kernels for 0% -> 0%
where the time goes in v1:
time: 1440 us; the launch traced here: 1430 us
  waiting for transfers between devices  765 us (53%)
  matrix products  349 us (24%)
  blocking collectives  119 us (8%)
  starting transfers between devices  74.9 us (5%)
  local copies, waits for them, and re-layouts  66.4 us (5%)
  other arithmetic  37 us (3%)
  between operations  17 us (1%)
    reduce_scatter x7, waiting for transfers between devices, per_device(): lax.psum_scatter(shortened(totals), ('dp', 'blk'), scatter_dimension=0, t...  351 us
    psum x1, waiting for transfers between devices, per_device(): lax.psum(shortened(owned), 'head')  179 us
    dot_general x14, matrix products, first_dot(): lax.dot_general(left, right, (((0,), (0,)), ((), ())), preferred_element_...  106 us
    dot_general x14, matrix products, last_dot(): lax.dot_general(left, right, (((1,), (1,)), ((), ())), preferred_element_...  76.6 us
    all_gather x1, waiting for transfers between devices, per_device(): down_w = lax.all_gather(shards[8], ('dp', 'blk'), axis=0, tiled=True)  66.3 us
    dot_general x14, matrix products, plain_dot(): return jnp.dot(left, right, preferred_element_type=jnp.float32)  63.4 us
    all_gather x1, waiting for transfers between devices, per_device(): up_w = lax.all_gather(shards[7], ('dp', 'blk'), axis=0, tiled=True)  55.4 us
    all_gather x2, blocking collectives, per_device(): key_piece = lax.all_gather(head_k, 'blk', axis=0, tiled=True)  34.1 us
  transfers between devices with their start and end apart: 35, of which 19 were waited for; matrix products, arithmetic and copies ran while one was open for 25% of the time, Pallas kernels for 0%

profile of v1, /device:TPU:0, one launch (start us, length us, event | category | flops | bytes accessed | tf_op | source)
XLA Modules:
  0.0 1429.8 jit_solution(1590820496180316066)
XLA Ops:
  13.7 16.3 %all-reduce.5 = (bf16[1536]{0:T(1024)(128)(2,1)S(1)}, bf16[1536]{0:T(1024)(128)(2,1)S(1)}) all-reduce(bf16[1536]{0:T(1024)(128)(2,1)S(1)} %dynamic-update-slice, bf16[1536]{0:T(1024)(128)(2,1)S(1)} %dynamic-update-slice.1), channel_id=1, replica_groups=mesh['dp'=2,'blk'=4,'head'=4] {'dp','blk'}, use_global_device_ids=true, to_apply=%add | all-reduce | flops 3072 | bytes 12288
  57.7 15.3 %all-gather.14.cloned.1.call-done = bf16[1536,768]{1,0:T(8,128)(2,1)} async-done(((bf16[192,768]{1,0:T(8,128)(2,1)}), bf16[1536,768]{1,0:T(8,128)(2,1)}) %all-gather.14.cloned.1.call-update) | async-done | bytes 2359312 | tf_op jit(solution)/shard_map/all_gather | solution.py:107
  105.3 13.9 all_gather.73
  119.3 14.7 %all_gather.74 = bf16[2048,2,96]{0,2,1:T(8,128)(2,1)} all-gather(bf16[512,2,96]{0,2,1:T(8,128)(2,1)S(1)} %all_to_all.200), channel_id=1, replica_groups=mesh['dp'=2,'blk'=4,'head'=4] {'blk'}, dimensions={0}, use_global_device_ids=true | all-gather | bytes 983040 | tf_op jit(solution)/shard_map/all_gather | solution.py:133
  144.5 20.2 %all_gather.63 = bf16[2048,2,96]{0,2,1:T(8,128)(2,1)} all-gather(bf16[512,2,96]{0,2,1:T(8,128)(2,1)S(1)} %all_to_all.179), channel_id=1, replica_groups=mesh['dp'=2,'blk'=4,'head'=4] {'blk'}, dimensions={0}, use_global_device_ids=true | all-gather | bytes 983040 | tf_op jit(solution)/shard_map/all_gather | solution.py:132
  164.9 11.3 all_gather.66
  258.6 55.4 %all-gather.20.cloned.1.call-done = bf16[1536,4096]{1,0:T(8,128)(2,1)} async-done(((bf16[192,4096]{1,0:T(8,128)(2,1)}), bf16[1536,4096]{1,0:T(8,128)(2,1)}) %all-gather.20.cloned.1.call-update) | async-done | bytes 12582928 | tf_op jit(solution)/shard_map/all_gather | solution.py:111
  321.7 66.3 %all-gather.22.cloned.1.call-done = bf16[4096,1536]{1,0:T(8,128)(2,1)} async-done(((bf16[512,1536]{1,0:T(8,128)(2,1)}), bf16[4096,1536]{1,0:T(8,128)(2,1)}) %all-gather.22.cloned.1.call-update) | async-done | bytes 12582928 | tf_op jit(solution)/shard_map/all_gather | solution.py:112
  388.0 11.4 multiply_convert_fusion.2
  399.4 10.5 fusion.216
  410.0 11.6 multiply_reduce_fusion.1
  432.3 9.9 multiply_convert_fusion
  442.2 9.8 fusion.218
  452.1 9.8 multiply_reduce_fusion
  489.4 50.1 %while.25 = (s32[]{:T(128)}, f32[1,512,2,2,96]{1,4,3,2,0:T(8,128)}, bf16[4,512,2,96]{1,3,2,0:T(8,128)(2,1)}, bf16[4,512,2,96]{1,3,2,0:T(8,128)(2,1)}, bf16[4,512...) while((s32[]{:T(128)}, f32[1,512,2,2,96]{1,4,3,2,0:T(8,128)}, ...), condition=%wide.region_18.19_spmd.clone, body=%wide.region_17.18_spmd.clone.sunk | while | flops 1018593792 | bytes 67217776 | solution.py:267
  545.3 46.3 %while.24 = (s32[]{:T(128)}, f32[1,512,2,2,96]{1,4,3,2,0:T(8,128)S(1)}, bf16[4,512,2,96]{1,3,2,0:T(8,128)(2,1)}, bf16[4,512,2,96]{1,3,2,0:T(8,128)(2,1)}, bf16[4...) while((s32[]{:T(128)}, ...), condition=%wide.region_11.12_spmd.clone, body=%wide.region_10.11_spmd.clone.sunk | while | flops 1018593792 | bytes 69314976 | solution.py:267
  604.1 16.3 %reduce-scatter.12.cloned.1.call-done = bf16[512,2,96]{0,2,1:T(8,128)(2,1)} async-done(((bf16[2048,2,96]{0,2,1:T(8,128)(2,1)}), bf16[512,2,96]{0,2,1:T(8,128)(2,1)}) %reduce-scatter.12.cloned.1.call-update) | async-done | bytes 196624 | tf_op jit(solution)/shard_map/reduce_scatter | solution.py:272
  639.3 10.6 reduce-scatter.18.cloned.1.call-done
  656.3 22.6 %reduce-scatter.14.cloned.1.call-done = bf16[512,2,96]{0,2,1:T(8,128)(2,1)} async-done(((bf16[2048,2,96]{0,2,1:T(8,128)(2,1)}), bf16[512,2,96]{0,2,1:T(8,128)(2,1)}) %reduce-scatter.14.cloned.1.call-update) | async-done | bytes 196624 | tf_op jit(solution)/shard_map/reduce_scatter | solution.py:275
  739.6 11.8 fusion.220
  751.4 14.9 %add_convert_fusion.2 = bf16[1536,4096]{1,0:T(8,128)(2,1)} fusion(f32[1536,4096]{1,0:T(8,128)} %fusion.220, bf16[128,1536]{1,0:T(8,128)(2,1)S(1)} %copy-done.16, bf16[128,4096]{1,0:T(8,128)(2,1)S(1)} %copy-done.37), kind=kOutput, calls=%fused_computation.80 | convolution fusion | flops 1623195648 | bytes 39190528 | tf_op jit(solution)/shard_map/dot_general | solution.py:28
  766.6 11.5 fusion.221
  778.1 16.7 %add_convert_fusion.1 = bf16[1536,4096]{1,0:T(8,128)(2,1)} fusion(f32[1536,4096]{1,0:T(8,128)} %fusion.221, bf16[128,1536]{1,0:T(8,128)(2,1)S(1)} %copy-done.16, bf16[128,4096]{1,0:T(8,128)(2,1)S(1)} %copy-done.35), kind=kOutput, calls=%fused_computation.79 | convolution fusion | flops 1623195648 | bytes 39190528 | tf_op jit(solution)/shard_map/dot_general | solution.py:28
  796.0 11.8 fusion.165
  807.8 15.0 %add_convert_fusion = bf16[4096,1536]{1,0:T(8,128)(2,1)} fusion(f32[4096,1536]{1,0:T(8,128)} %fusion.165, bf16[128,4096]{1,0:T(8,128)(2,1)S(1)} %copy-done.25, bf16[2,1,128,1536]{3,2,1,0:T(8,128)(2,1)S(1)} %copy-done.45), kind=kOutput, calls=%fused_computation.78 | convolution fusion | flops 1623195648 | bytes 39190528 | tf_op jit(solution)/shard_map/dot_general | solution.py:28
  829.2 57.6 %reduce-scatter.20.cloned.1.call-done = bf16[192,1536]{1,0:T(8,128)(2,1)} async-done(((bf16[1536,1536]{1,0:T(8,128)(2,1)}), bf16[192,1536]{1,0:T(8,128)(2,1)}) %reduce-scatter.20.cloned.1.call-update) | async-done | bytes 589840 | tf_op jit(solution)/shard_map/reduce_scatter | solution.py:327
  886.8 95.8 %reduce-scatter.28.cloned.1.call-done = bf16[192,4096]{1,0:T(8,128)(2,1)} async-done(((bf16[1536,4096]{1,0:T(8,128)(2,1)}), bf16[192,4096]{1,0:T(8,128)(2,1)}) %reduce-scatter.28.cloned.1.call-update) | async-done | bytes 1572880 | tf_op jit(solution)/shard_map/reduce_scatter | solution.py:327
  982.6 95.8 %reduce-scatter.30.cloned.1.call-done = bf16[192,4096]{1,0:T(8,128)(2,1)} async-done(((bf16[1536,4096]{1,0:T(8,128)(2,1)}), bf16[192,4096]{1,0:T(8,128)(2,1)}) %reduce-scatter.30.cloned.1.call-update) | async-done | bytes 1572880 | tf_op jit(solution)/shard_map/reduce_scatter | solution.py:327
  1078.4 95.8 %reduce-scatter.32.cloned.1.call-done = bf16[512,1536]{1,0:T(8,128)(2,1)} async-done(((bf16[4096,1536]{1,0:T(8,128)(2,1)}), bf16[512,1536]{1,0:T(8,128)(2,1)}) %reduce-scatter.32.cloned.1.call-update) | async-done | bytes 1572880 | tf_op jit(solution)/shard_map/reduce_scatter | solution.py:327
  1198.3 14.9 %all-reduce.4 = (bf16[1536]{0:T(1024)(128)(2,1)S(1)}, bf16[1536]{0:T(1024)(128)(2,1)S(1)}) all-reduce(bf16[1536]{0:T(1024)(128)(2,1)S(1)} %add_convert_fusion.6, bf16[1536]{0:T(1024)(128)(2,1)S(1)} %add_convert_fusion.5), channel_id=8, replica_groups=mesh['dp'=2,'blk'=4,'head'=4] {'dp','blk'}, use_global_device_ids=true, to_apply=%region_24.25.clone | all-reduce | flops 3072 | bytes 12288
  1213.3 12.2 all-reduce.6
  1229.2 179.4 %all-reduce.10.cloned.1.call-done = (bf16[192,1536]{1,0:T(8,128)(2,1)}, bf16[192,768]{1,0:T(8,128)(2,1)}, bf16[192,768]{1,0:T(8,128)(2,1)}, bf16[192,1536]{1,0:T...) async-done(((bf16[192,1536]{1,0:T(8,128)(2,1)}, bf16[192,768]{1,0:T(8,128)(2,1)}, bf16[192,768]{1,0:T(8,128)(2,1)}, ...) | async-done | bytes 6488080 | tf_op jit(solution)/shard_map/psum | solution.py:329
  (567 shorter events, 452.5 us)
Async XLA Ops:
  7.2 42.5 %all-gather.10.cloned.1.call-start = ((), (), s32[]{:S(2)}) async-start(), calls=%async_computation.27 | async-start | bytes 2654208 | tf_op jit(solution)/shard_map/all_gather | solution.py:106
  8.0 65.1 %all-gather.14.cloned.1.call-start = ((), (), s32[]{:S(2)}) async-start(), calls=%async_computation.29 | async-start | bytes 2654208 | tf_op jit(solution)/shard_map/all_gather | solution.py:107
  8.7 125.2 %all-gather.12.cloned.1.call-start = ((), (), s32[]{:S(2)}) async-start(), calls=%async_computation.28 | async-start | bytes 5308416 | tf_op jit(solution)/shard_map/all_gather | solution.py:105
  9.5 234.9 %all-gather.16.cloned.1.call-start = ((), (), s32[]{:S(2)}) async-start(), calls=%async_computation.30 | async-start | bytes 5308416 | tf_op jit(solution)/shard_map/all_gather | solution.py:108
  10.0 240.1 %all-gather.18.cloned.1.call-start = ((), (), s32[]{:S(2)}) async-start(), calls=%async_computation.31 | async-start | bytes 14155776 | tf_op jit(solution)/shard_map/all_gather | solution.py:110
  10.6 303.4 %all-gather.20.cloned.1.call-start = ((), (), s32[]{:S(2)}) async-start(), calls=%async_computation.32 | async-start | bytes 14155776 | tf_op jit(solution)/shard_map/all_gather | solution.py:111
  11.2 376.8 %all-gather.22.cloned.1.call-start = ((), (), s32[]{:S(2)}) async-start(), calls=%async_computation.33 | async-start | bytes 14155776 | tf_op jit(solution)/shard_map/all_gather | solution.py:112
  52.8 25.0 %all-to-all-start.4 = ((bf16[128,8,96]{0,2,1:T(8,128)(2,1)}), bf16[128,8,96]{0,2,1:T(8,128)(2,1)S(1)}, u32[]{:S(2)}, u32[]{:S(2)}) async-start(bf16[128,8,96]{0,2,1:T(8,128)(2,1)} %bitcast.29), calls=%async_computation.4 | async-start | bytes 393216 | tf_op jit(solution)/shard_map/all_to_all | solution.py:125
  100.8 37.3 %all-to-all-start.2 = ((bf16[128,8,96]{0,2,1:T(8,128)(2,1)}), bf16[128,8,96]{0,2,1:T(8,128)(2,1)S(1)}, u32[]{:S(2)}, u32[]{:S(2)}) async-start(bf16[128,8,96]{0,2,1:T(8,128)(2,1)} %bitcast.13), calls=%async_computation.2 | async-start | bytes 393216 | tf_op jit(solution)/shard_map/all_to_all | solution.py:126
  138.0 44.7 %all-to-all-start.5 = ((bf16[128,16,96]{0,2,1:T(8,128)(2,1)}), bf16[128,16,96]{0,2,1:T(8,128)(2,1)S(1)}, u32[]{:S(2)}, u32[]{:S(2)}) async-start(bf16[128,16,96]{0,2,1:T(8,128)(2,1)} %bitcast.34), calls=%async_computation.5 | async-start | bytes 786432 | tf_op jit(solution)/shard_map/all_to_all | solution.py:124
  182.8 22.0 %all-to-all-start.1 = ((bf16[128,16,96]{0,2,1:T(8,128)(2,1)}), bf16[128,16,96]{0,2,1:T(8,128)(2,1)}, u32[]{:S(2)}, u32[]{:S(2)}) async-start(bf16[128,16,96]{0,2,1:T(8,128)(2,1)} %bitcast.9), calls=%async_computation.1 | async-start | bytes 786432 | tf_op jit(solution)/shard_map/all_to_all | solution.py:124
  204.7 22.1 %all-to-all-start.7 = ((bf16[512,4,96]{2,1,0:T(4,128)(2,1)}), bf16[512,4,96]{2,1,0:T(4,128)(2,1)S(1)}, u32[]{:S(2)}, u32[]{:S(2)}) async-start(bf16[512,4,96]{2,1,0:T(4,128)(2,1)} %copy.188), calls=%async_computation.7 | async-start | bytes 1048576 | tf_op jit(solution)/shard_map/all_to_all | solution.py:178
  226.9 16.0 %all-to-all-start.3 = ((bf16[512,4,96]{2,1,0:T(4,128)(2,1)}), bf16[512,4,96]{2,1,0:T(4,128)(2,1)}, u32[]{:S(2)}, u32[]{:S(2)}) async-start(bf16[512,4,96]{2,1,0:T(4,128)(2,1)} %copy.178), calls=%async_computation.3 | async-start | bytes 1048576 | tf_op jit(solution)/shard_map/all_to_all | solution.py:178
  464.9 16.7 %all-to-all-start.12 = ((bf16[128,16,96]{0,2,1:T(8,128)(2,1)}), bf16[128,16,96]{0,2,1:T(8,128)(2,1)S(1)}, u32[]{:S(2)}, u32[]{:S(2)}) async-start(bf16[128,16,96]{0,2,1:T(8,128)(2,1)} %bitcast.79), calls=%async_computation.14 | async-start | bytes 786432 | tf_op jit(solution)/shard_map/all_to_all | solution.py:206
  481.6 60.2 %all-to-all-start.8 = ((bf16[128,16,96]{0,2,1:T(8,128)(2,1)}), bf16[128,16,96]{0,2,1:T(8,128)(2,1)}, u32[]{:S(2)}, u32[]{:S(2)}) async-start(bf16[128,16,96]{0,2,1:T(8,128)(2,1)} %bitcast.57), calls=%async_computation.8 | async-start | bytes 786432 | tf_op jit(solution)/shard_map/all_to_all | solution.py:206
  485.7 111.4 %reduce-scatter.16.cloned.1.call-start = ((), (), s32[]{:S(2)}) async-start(), calls=%async_computation.36 | async-start | bytes 983040 | tf_op jit(solution)/shard_map/reduce_scatter | solution.py:272
  541.8 78.7 %reduce-scatter.12.cloned.1.call-start = ((), (), s32[]{:S(2)}) async-start(), calls=%async_computation.34 | async-start | bytes 983040 | tf_op jit(solution)/shard_map/reduce_scatter | solution.py:272
  593.8 56.1 %reduce-scatter.18.cloned.1.call-start = ((), (), s32[]{:S(2)}) async-start(), calls=%async_computation.37 | async-start | bytes 983040 | tf_op jit(solution)/shard_map/reduce_scatter | solution.py:275
  596.1 82.8 %reduce-scatter.14.cloned.1.call-start = ((), (), s32[]{:S(2)}) async-start(), calls=%async_computation.35 | async-start | bytes 983040 | tf_op jit(solution)/shard_map/reduce_scatter | solution.py:275
  599.0 23.3 %all-to-all-start.14 = ((bf16[512,2,96]{2,1,0:T(2,128)(2,1)}), bf16[512,2,96]{2,1,0:T(2,128)(2,1)S(1)}, u32[]{:S(2)}, u32[]{:S(2)}) async-start(bf16[512,2,96]{2,1,0:T(2,128)(2,1)} %copy.208), calls=%async_computation.17 | async-start | bytes 524288 | tf_op jit(solution)/shard_map/all_to_all | solution.py:280
  622.3 13.5 all-to-all-start.10
  626.9 196.2 %reduce-scatter.22.cloned.1.call-start = ((), (), s32[]{:S(2)}) async-start(), calls=%async_computation.39 | async-start | bytes 2654208 | tf_op jit(solution)/shard_map/reduce_scatter | solution.py:327
  651.7 29.0 %all-to-all-start.15 = ((bf16[512,2,96]{2,1,0:T(2,128)(2,1)}), bf16[512,2,96]{2,1,0:T(2,128)(2,1)S(1)}, u32[]{:S(2)}, u32[]{:S(2)}) async-start(bf16[512,2,96]{2,1,0:T(2,128)(2,1)} %copy.212), calls=%async_computation.19 | async-start | bytes 524288 | tf_op jit(solution)/shard_map/all_to_all | solution.py:283
  680.7 13.5 all-to-all-start.11
  685.3 137.8 %reduce-scatter.24.cloned.1.call-start = ((), (), s32[]{:S(2)}) async-start(), calls=%async_computation.40 | async-start | bytes 2654208 | tf_op jit(solution)/shard_map/reduce_scatter | solution.py:327
  697.7 131.5 %reduce-scatter.26.cloned.1.call-start = ((), (), s32[]{:S(2)}) async-start(), calls=%async_computation.41 | async-start | bytes 5308416 | tf_op jit(solution)/shard_map/reduce_scatter | solution.py:327
  704.1 13.8 all-to-all-start.9
  721.3 165.4 %reduce-scatter.20.cloned.1.call-start = ((), (), s32[]{:S(2)}) async-start(), calls=%async_computation.38 | async-start | bytes 5308416 | tf_op jit(solution)/shard_map/reduce_scatter | solution.py:327
  738.6 244.0 %reduce-scatter.28.cloned.1.call-start = ((), (), s32[]{:S(2)}) async-start(), calls=%async_computation.42 | async-start | bytes 14155776 | tf_op jit(solution)/shard_map/reduce_scatter | solution.py:327
  766.4 312.0 %reduce-scatter.30.cloned.1.call-start = ((), (), s32[]{:S(2)}) async-start(), calls=%async_computation.43 | async-start | bytes 14155776 | tf_op jit(solution)/shard_map/reduce_scatter | solution.py:327
  794.9 379.3 %reduce-scatter.32.cloned.1.call-start = ((), (), s32[]{:S(2)}) async-start(), calls=%async_computation.44 | async-start | bytes 14155776 | tf_op jit(solution)/shard_map/reduce_scatter | solution.py:327
  822.8 585.8 %all-reduce.10.cloned.1.call-start = ((), (), s32[]{:S(2)}) async-start(), calls=%async_computation.45 | async-start | bytes 12976128 | tf_op jit(solution)/shard_map/psum | solution.py:329
  (139 other events, 2662.6 us)
Sparse Core Ops, SparseCore 0:
  9.9 32.1 all-gather.9
  44.0 28.9 all-gather.13
  75.0 42.0 all-gather.11
  118.8 46.9 all-gather.15
  167.6 72.4 all-gather.17
  241.8 72.1 all-gather.19
  315.9 72.1 all-gather.21
  541.9 26.5 reduce-scatter.15
  593.9 26.4 reduce-scatter.11
  623.8 26.0 reduce-scatter.17
  652.8 26.0 reduce-scatter.13
  682.7 42.4 reduce-scatter.21
  729.5 42.4 reduce-scatter.23
  775.3 53.8 reduce-scatter.25
  832.9 53.8 reduce-scatter.19
  890.1 92.3 reduce-scatter.27
  985.9 92.3 reduce-scatter.29
  1081.7 92.3 reduce-scatter.31
  1177.1 231.4 all-reduce.9
